TPU v7x, 128 devices: a whole 4x4x4 slice. The times are simulated.
128 devices in a mesh: rep: 4 (over y), exp: 32 (over x, z, core).
Axes of the slice: x: 4, y: 4, z: 4, core: 2. Of those that a mesh axis runs over, the one named last changes fastest.
Arguments:
- tokens: bfloat16 [16384, 3584], P(('rep', 'exp')), parts along dimension 0, may hold values from -6 to 6
- expert_ids: int32 [16384, 4], P(('rep', 'exp')), parts along dimension 0, may hold values from 0 to 31, all different within a row; in each aligned block of 128 rows (0 to 127, 128 to 255, ...) at most 24 rows name the same one
- gate_probs: float32 [16384, 4], P(('rep', 'exp')), parts along dimension 0, may hold values from 0.1 to 1
- placed: int32 [32], replicated, may hold values from 0 to 31, each once
- w_gate: bfloat16 [32, 3584, 1024], P('exp'), may hold values from -0.09375 to 0.09375
- w_up: bfloat16 [32, 3584, 1024], P('exp'), may hold values from -0.09375 to 0.09375
- w_down: bfloat16 [32, 1024, 3584], P('exp'), may hold values from -0.1875 to 0.1875
Outputs:
- mixed: bfloat16 [16384, 3584], P(('rep', 'exp')), parts along dimension 0
There are 4 independent parts, one for each index of `rep`. A program takes and returns all parts, laid end to end along the dimension named above; an argument that names none is the same for every part. Nothing has to cross between parts.
Inputs may be any that keep to these rules, and one draw needn't show every extreme that they name: `expert_ids`: each row names 4 different experts. In the rows of one device no expert is named more than 24 times, a bound that some block reaches. `placed`: each expert once.
All inputs are finite; a program needn't handle non-finite values.
Results may differ from a plain program's by a relative error of at most 0.008.
Values may be sent and summed in bfloat16 or wider, within the bound.
A program may use at most 192 MiB of HBM per device.

v0:
```python
import jax
import jax.numpy as jnp
from jax import lax
from jax.sharding import PartitionSpec as P


def expert_rows(rows, gate_w, up_w, down_w):
    gate = jnp.dot(rows, gate_w, preferred_element_type=jnp.float32)
    up = jnp.dot(rows, up_w, preferred_element_type=jnp.float32)
    hidden = (jax.nn.silu(gate) * up).astype(jnp.bfloat16)
    return jnp.dot(hidden, down_w, preferred_element_type=jnp.float32).astype(jnp.bfloat16)


def run_expert(received, gate_w, up_w, down_w):
    sources, room, width = received.shape
    total_rows = sources * room
    flat = received.reshape(total_rows, width)
    result = expert_rows(flat, gate_w, up_w, down_w)
    return result.reshape(sources, room, width)


def body(tokens, expert_ids, gate_probs, placed, w_gate, w_up, w_down):
    tok_rows, width = tokens.shape
    picks = expert_ids.shape[1]
    devices = lax.axis_size("exp")
    average = tok_rows * picks // devices
    room = average + max(1, tok_rows * picks // (2 * devices))
    gate_w, up_w, down_w = (w_gate[0], w_up[0], w_down[0])
    numbers = jnp.arange(devices, dtype=jnp.int32)
    home = jnp.sum(jnp.where(placed[None, :] == numbers[:, None], numbers[None, :], 0), axis=1)
    flat_ids = expert_ids.reshape(-1)
    target_dev = jnp.take(home, flat_ids)
    one_hot = (target_dev[:, None] == numbers[None, :]).astype(jnp.int32)
    rank = jnp.sum((jnp.cumsum(one_hot, axis=0) - 1) * one_hot, axis=1)
    slot_index = target_dev * room + rank
    owner = jnp.arange(tok_rows * picks, dtype=jnp.int32) // picks
    slot_tok = jnp.full((devices * room,), tok_rows, jnp.int32).at[slot_index].set(owner)
    outgoing = jnp.take(tokens, slot_tok, axis=0, mode="fill", fill_value=0).reshape(
        devices, room, width
    )
    received = lax.all_to_all(outgoing, "exp", split_axis=0, concat_axis=0, tiled=True)
    produced = run_expert(received, gate_w, up_w, down_w)
    returned = lax.all_to_all(produced, "exp", split_axis=0, concat_axis=0, tiled=True)
    picked = jnp.take(returned.reshape(devices * room, width), slot_index, axis=0)
    picked = picked.reshape(tok_rows, picks, width)
    mixed = jnp.einsum("tk,tkd->td", gate_probs, picked.astype(jnp.float32))
    return mixed.astype(jnp.bfloat16)


def solution(mesh):
    return jax.shard_map(
        body,
        mesh=mesh,
        in_specs=(
            P(("rep", "exp"), None),
            P(("rep", "exp"), None),
            P(("rep", "exp"), None),
            P(),
            P("exp", None, None),
            P("exp", None, None),
            P("exp", None, None),
        ),
        out_specs=P(("rep", "exp"), None),
        check_vma=False,
    )
```

profile of v0, /device:TPU:32, one launch (start us, length us, event | category | flops | bytes accessed | tf_op | source)
XLA Modules:
  0.0 242.7 jit_solution(17339483279401050000)
XLA Ops:
  0.0 0.0 copy-start
  0.0 0.8 select_reduce_fusion
  0.9 0.7 fusion.29
  1.6 0.7 fusion.28
  2.3 0.8 copy.27
  3.1 0.1 reshape.155
  3.2 0.1 reshape.156
  3.3 0.1 reshape.157
  3.4 4.4 %compare_select_fusion.3 = (s32[512,1]{0,1:T(1,128)S(1)}, s32[512,1]{0,1:T(1,128)S(1)}) fusion(s32[]{:T(128)} %bitcast.25, s32[]{:T(128)} %bitcast.26, s32[]{:T(128)} %bitcast.27, s32[]{:T(128)} %bitcast.28, s32[]{:T(128)} %bitcast.29, s32[]{:T(128)} %bitcast.31, s32[]{:T(128)} %bitcast.30, s32[512,1]{0,1:T(1,128)S(1)} %reshape.155), kind=kLoop, calls=%fused_computation.56 | loop fusion | flops 7680 | bytes 6172 | tf_op jit(solution)/shard_map/jit(_take)/gather | solution.py:32
  7.8 0.2 compare_reduce_fusion.24
  8.0 15.7 %and_select_fusion.1 = (s32[512]{0:T(512)S(1)}, s32[512]{0:T(512)S(1)}) fusion(s32[512]{0:T(512)S(1)} %reshape.156, pred[512]{0:T(512)(128)(4,1)S(1)} %get-tuple-element.29, pred[512]{0:T(512)(128)(4,1)S(1)} %get-tuple-element.27, pred[512]{0:T(512)(128)(4,1)S(1)} %get-tuple-element.28, pred[512]{0:T(512)(128)(4,1)S(1)} %get-tuple-element.26, ...), kind=kLoop, calls=%fused_computation.82 | loop fusion | flops 16384 | bytes 21092 | tf_op jit(solution)/shard_map/jit(_take)/select_n | solution.py:32
  23.7 1.2 reduce-window.6
  24.9 0.2 slice_reduce_fusion
  25.1 0.1 fusion.19
  25.3 2.4 %scatter_custom_fusion = s32[768]{0:T(1024)S(1)} fusion(s32[512]{0:T(512)S(1)} %bitcast.86, s32[512]{0:T(512)S(1)} %add_select_fusion, s32[]{:T(128)} %constant.70.clone.1), kind=kCustom, calls=%fused_computation.78 | custom fusion | bytes 3076 | tf_op jit(solution)/shard_map/scatter | solution.py:37
  27.8 0.1 broadcast_in_dim.65
  27.9 0.0 copy-done
  27.9 5.4 %gather_fusion = bf16[768,3584]{1,0:T(8,128)(2,1)} fusion(bf16[128,3584]{1,0:T(8,128)(2,1)S(1)} %copy-done, s32[1024]{0:T(1024)S(1)} %pad_clamp_fusion.1), kind=kCustom, calls=%fused_computation | custom fusion | bytes 11013120 | tf_op jit(solution)/shard_map/jit(_take)/gather | solution.py:38
  33.3 3.0 %broadcast_select_fusion = bf16[32,24,3584]{2,1,0:T(8,128)(2,1)S(1)} fusion(bf16[32,24,3584]{2,1,0:T(8,128)(2,1)} %bitcast.79, pred[32,24]{1,0:T(8,128)(4,1)S(1)} %broadcast_in_dim.65), kind=kLoop, calls=%fused_computation.10 | loop fusion | flops 2752512 | bytes 11010816 | tf_op jit(solution)/shard_map/jit(_take)/select_n | solution.py:38
  36.3 0.0 copy-start.4
  36.3 71.6 %all_to_all.10 = bf16[32,24,3584]{2,1,0:T(8,128)(2,1)S(1)} all-to-all(bf16[32,24,3584]{2,1,0:T(8,128)(2,1)S(1)} %broadcast_select_fusion), channel_id=1, replica_groups=mesh['rep'=4,'exp'=32] {'exp'}, dimensions={0} | all-to-all | bytes 11010048 | tf_op jit(solution)/shard_map/all_to_all | solution.py:41
  108.0 0.0 copy-start.1
  108.0 2.5 %copy-done.1 = bf16[32,24,3584]{2,1,0:T(8,128)(2,1)} copy-done((bf16[32,24,3584]{2,1,0:T(8,128)(2,1)}, bf16[32,24,3584]{2,1,0:T(8,128)(2,1)S(1)}, u32[]{:S(2)}) %copy-start.1) | copy-done | bytes 5505048
  110.4 0.0 copy-done.4
  110.4 7.6 %fusion.2 = f32[768,1024]{1,0:T(8,128)} fusion(bf16[768,3584]{1,0:T(8,128)(2,1)S(1)} %bitcast.81, bf16[1,3584,1024]{2,1,0:T(8,128)(2,1)S(1)} %copy-done.4), kind=kOutput, calls=%fused_computation.5 | convolution fusion | flops 5637144576 | bytes 15990784 | tf_op jit(solution)/shard_map/dot_general | solution.py:9
  118.0 20.0 %fusion.6 = bf16[768,3584]{1,0:T(8,128)(2,1)} fusion(bf16[1,1024,3584]{2,1,0:T(8,128)(2,1)} %param.13, f32[768,1024]{1,0:T(8,128)} %fusion.2, bf16[768,3584]{1,0:T(8,128)(2,1)} %bitcast.82, bf16[1,3584,1024]{2,1,0:T(8,128)(2,1)} %param.11), kind=kOutput, calls=%fused_computation.9 | convolution fusion | flops 11281760256 | bytes 28835840 | tf_op jit(solution)/shard_map/dot_general | solution.py:11
  138.0 0.0 copy-start.2
  138.0 0.0 copy-start.3
  138.0 6.6 %all-to-all-start.1 = ((bf16[32,24,3584]{2,1,0:T(8,128)(2,1)}), bf16[32,24,3584]{2,1,0:T(8,128)(2,1)}, u32[]{:S(2)}, u32[]{:S(2)}) async-start(bf16[32,24,3584]{2,1,0:T(8,128)(2,1)} %bitcast.80), calls=%async_computation.1 | async-start | bytes 11010048 | tf_op jit(solution)/shard_map/all_to_all | solution.py:43
  144.6 0.1 reduce_sum.24
  144.7 0.1 gather.23
  144.8 0.1 copy.32
  144.9 0.1 copy.28
  145.0 0.0 copy-done.2
  145.0 0.1 copy.33
  145.2 0.0 copy-done.3
  145.2 0.2 copy.34
  145.3 74.0 %all-to-all-done.1 = bf16[32,24,3584]{2,1,0:T(8,128)(2,1)} async-done(((bf16[32,24,3584]{2,1,0:T(8,128)(2,1)}), bf16[32,24,3584]{2,1,0:T(8,128)(2,1)}, u32[]{:S(2)}, u32[]{:S(2)}) %all-to-all-start.1) | async-done | bytes 5505056 | tf_op jit(solution)/shard_map/all_to_all | solution.py:43
  219.3 11.2 %gather_fusion.1 = bf16[512,3584]{1,0:T(8,128)(2,1)} fusion(bf16[768,3584]{1,0:T(8,128)(2,1)} %bitcast.44, s32[1024]{0:T(1024)S(1)} %pad_clamp_fusion), kind=kCustom, calls=%fused_computation.1 | custom fusion | bytes 7342080 | tf_op jit(solution)/shard_map/jit(_take)/gather | solution.py:44
  230.5 7.0 %gather.29 = bf16[128,4,3584]{2,1,0:T(4,128)(2,1)} reshape(bf16[512,3584]{1,0:T(8,128)(2,1)} %gather_fusion.1) | data formatting | bytes 7340032 | tf_op jit(solution)/shard_map/jit(_take)/gather | solution.py:44
  237.5 4.2 %fusion.9 = bf16[128,1,3584]{2,1,0:T(2,128)(2,1)S(1)} fusion(bf16[128,4,1]{1,2,0:T(2,128)(2,1)S(1)} %copy.34, bf16[128,4,3584]{2,1,0:T(4,128)(2,1)} %gather.29, pred[128,4]{1,0:T(8,128)(4,1)S(1)} %copy.33), kind=kOutput, calls=%fused_computation.11 | convolution fusion | flops 5505024 | bytes 4589056 | tf_op jit(solution)/shard_map/tk,tkd->td/dot_general | solution.py:46
  241.7 1.0 copy.39
  (11 shorter events, 0.1 us)
Async XLA Ops:
  0.0 27.9 %copy-start = (bf16[128,3584]{1,0:T(8,128)(2,1)S(1)}, bf16[128,3584]{1,0:T(8,128)(2,1)}, u32[]{:S(2)}) copy-start(bf16[128,3584]{1,0:T(8,128)(2,1)} %param.7) | copy-start | bytes 2752516
  36.3 74.1 %copy-start.4 = (bf16[1,3584,1024]{2,1,0:T(8,128)(2,1)S(1)}, bf16[1,3584,1024]{2,1,0:T(8,128)(2,1)}, u32[]{:S(2)}) copy-start(bf16[1,3584,1024]{2,1,0:T(8,128)(2,1)} %param.12) | copy-start | bytes 22020100
  108.0 2.5 %copy-start.1 = (bf16[32,24,3584]{2,1,0:T(8,128)(2,1)}, bf16[32,24,3584]{2,1,0:T(8,128)(2,1)S(1)}, u32[]{:S(2)}) copy-start(bf16[32,24,3584]{2,1,0:T(8,128)(2,1)S(1)} %all_to_all.10) | copy-start | bytes 16515076
  138.0 7.0 %copy-start.2 = (s32[128,4]{0,1:T(4,128)S(1)}, s32[128,4]{0,1:T(4,128)}, u32[]{:S(2)}) copy-start(s32[128,4]{0,1:T(4,128)} %param.8) | copy-start | bytes 6148
  138.0 7.2 %copy-start.3 = (f32[128,4]{0,1:T(4,128)S(1)}, f32[128,4]{0,1:T(4,128)}, u32[]{:S(2)}) copy-start(f32[128,4]{0,1:T(4,128)} %param.9) | copy-start | bytes 6148
  138.0 81.3 %all-to-all-start.1 = ((bf16[32,24,3584]{2,1,0:T(8,128)(2,1)}), bf16[32,24,3584]{2,1,0:T(8,128)(2,1)}, u32[]{:S(2)}, u32[]{:S(2)}) async-start(bf16[32,24,3584]{2,1,0:T(8,128)(2,1)} %bitcast.80), calls=%async_computation.1 | async-start | bytes 11010048 | tf_op jit(solution)/shard_map/all_to_all | solution.py:43
where the time goes:
time: 243 us
  waiting for transfers between devices  74 us (30%)
  blocking collectives  71.6 us (29%)
  local copies, waits for them, and re-layouts  33.1 us (14%)
  matrix products  31.8 us (13%)
  other arithmetic  25.5 us (10%)
  starting transfers between devices  6.6 us (3%)
    all_to_all x1, waiting for transfers between devices, body(): lax.all_to_all(produced, 'exp', split_axis=0, concat_axis=0, tiled=True)  74 us
    all_to_all x1, blocking collectives, body(): lax.all_to_all(outgoing, 'exp', split_axis=0, concat_axis=0, tiled=True)  71.6 us
    dot_general x1, matrix products, expert_rows(): jnp.dot(hidden, down_w, preferred_element_type=jnp.float32)  20 us
    gather x2, local copies, waits for them, and re-layouts, body(): jnp.take(returned.reshape(devices * room, width), slot_index, axis=0)  18.2 us
    select_n x2, other arithmetic, body(): target_dev = jnp.take(home, flat_ids)  15.7 us
    dot_general x1, matrix products, expert_rows(): up = jnp.dot(rows, up_w, preferred_element_type=jnp.float32)  7.58 us
    all_to_all x1, starting transfers between devices, body(): lax.all_to_all(produced, 'exp', split_axis=0, concat_axis=0, tiled=True)  6.6 us
    gather x1, local copies, waits for them, and re-layouts, body(): jnp.take(tokens, slot_tok, axis=0, mode='fill', fill_value=0)  5.43 us
  transfers between devices with their start and end apart: 1, of which 1 were waited for; matrix products, arithmetic and copies ran while one was open for 0% of the time, Pallas kernels for 0%

commit v1 on v0

v1 whole, which is shorter than its diff:
```python
import jax
import jax.numpy as jnp
from jax import lax
from jax.sharding import PartitionSpec as P

ROOM = 24


def body(tokens, expert_ids, gate_probs, placed, w_gate, w_up, w_down):
    rows, width = tokens.shape
    devices = lax.axis_size("exp")
    hit = placed[:, None, None] == expert_ids[None, :, :]
    named = jnp.any(hit, axis=2)
    weight = jnp.sum(jnp.where(hit, gate_probs[None, :, :], 0.0), axis=2)
    t = jnp.arange(rows, dtype=jnp.int32)
    before = (t[:, None] < t[None, :]).astype(jnp.bfloat16)
    rank = jnp.dot(named.astype(jnp.bfloat16), before, preferred_element_type=jnp.float32)
    rank = jnp.where(named, rank, -1.0).astype(jnp.int32)
    slot = jnp.arange(ROOM, dtype=jnp.int32)
    chosen = rank[:, None, :] == slot[None, :, None]
    pick = chosen.astype(jnp.bfloat16).reshape(devices * ROOM, rows)
    outgoing = jnp.dot(pick, tokens, preferred_element_type=jnp.float32).astype(jnp.bfloat16)
    received = lax.all_to_all(outgoing.reshape(devices, ROOM, width), "exp", 0, 0, tiled=True)
    flat = received.reshape(devices * ROOM, width)
    gate = jnp.dot(flat, w_gate[0], preferred_element_type=jnp.float32)
    up = jnp.dot(flat, w_up[0], preferred_element_type=jnp.float32)
    hidden = (jax.nn.silu(gate) * up).astype(jnp.bfloat16)
    produced = jnp.dot(hidden, w_down[0], preferred_element_type=jnp.float32).astype(jnp.bfloat16)
    returned = lax.all_to_all(produced.reshape(devices, ROOM, width), "exp", 0, 0, tiled=True)
    high = weight.astype(jnp.bfloat16)
    low = (weight - high.astype(jnp.float32)).astype(jnp.bfloat16)
    zero = jnp.zeros((), jnp.bfloat16)
    mix_h = jnp.where(chosen, high[:, None, :], zero).reshape(devices * ROOM, rows)
    mix_l = jnp.where(chosen, low[:, None, :], zero).reshape(devices * ROOM, rows)
    back = returned.reshape(devices * ROOM, width)
    dims = (((0,), (0,)), ((), ()))
    mixed = lax.dot_general(mix_h, back, dims, preferred_element_type=jnp.float32)
    mixed = mixed + lax.dot_general(mix_l, back, dims, preferred_element_type=jnp.float32)
    return mixed.astype(jnp.bfloat16)


def solution(mesh):
    return jax.shard_map(
        body,
        mesh=mesh,
        in_specs=(
            P(("rep", "exp"), None),
            P(("rep", "exp"), None),
            P(("rep", "exp"), None),
            P(),
            P("exp", None, None),
            P("exp", None, None),
            P("exp", None, None),
        ),
        out_specs=P(("rep", "exp"), None),
        check_vma=False,
    )
```

time: 243 us -> 194 us (0.80)
  local copies, waits for them, and re-layouts: 33.1 us -> 2.59 us
  other arithmetic: 25.5 us -> 1.1 us
  matrix products: 31.8 us -> 37.2 us
    gather x7 -> x0, local copies, waits for them, and re-layouts: 25.2 us -> none  [the longest x2 18.2 us: body(): jnp.take(returned.reshape(devices * room, width), slot_index, axis=0)]
    select_n x6 -> x0, other arithmetic: 18.7 us -> none  [the longest x2 15.7 us: body(): target_dev = jnp.take(home, flat_ids)]
    dot_general x3 -> x6, matrix products: 31.8 us -> 37.2 us  [the longest x1 20 us: body(): jnp.dot(hidden, w_down[0], preferred_element_type=jnp.float32)]
    gather x4 -> x0, other arithmetic: 4.54 us -> none  [the longest x2 4.53 us: body(): target_dev = jnp.take(home, flat_ids)]
    scatter x1 -> x0, local copies, waits for them, and re-layouts: 2.45 us -> none  [body(): jnp.full((devices * room,), tok_rows, jnp.int32).at[slot_index].set(owner)]
where the time goes in v1:
time: 194 us
  waiting for transfers between devices  74.6 us (38%)
  blocking collectives  71.6 us (37%)
  matrix products  37.2 us (19%)
  starting transfers between devices  6.41 us (3%)
  local copies, waits for them, and re-layouts  2.59 us (1%)
    all_to_all x1, waiting for transfers between devices, body(): lax.all_to_all(produced.reshape(devices, ROOM, width), 'exp', 0, 0, tiled...  74.6 us
    all_to_all x1, blocking collectives, body(): lax.all_to_all(outgoing.reshape(devices, ROOM, width), 'exp', 0, 0, tiled...  71.6 us
    dot_general x1, matrix products, body(): jnp.dot(hidden, w_down[0], preferred_element_type=jnp.float32)  20 us
    dot_general x1, matrix products, body(): up = jnp.dot(flat, w_up[0], preferred_element_type=jnp.float32)  7.58 us
    all_to_all x1, starting transfers between devices, body(): lax.all_to_all(produced.reshape(devices, ROOM, width), 'exp', 0, 0, tiled...  6.41 us
    dot_general x1, matrix products, body(): lax.dot_general(mix_h, back, dims, preferred_element_type=jnp.float32)  4.4 us
  transfers between devices with their start and end apart: 1, of which 1 were waited for; matrix products, arithmetic and copies ran while one was open for 0% of the time, Pallas kernels for 0%

profile of v1, /device:TPU:32, one launch (start us, length us, event | category | flops | bytes accessed | tf_op | source)
XLA Modules:
  0.0 193.6 jit_solution(12839272137950561859)
XLA Ops:
  0.0 0.0 copy-start
  0.0 0.8 compare_reduce_fusion
  0.8 0.1 fusion.16
  1.0 0.1 eq.45
  1.1 0.2 bitcast_compare_fusion
  1.3 0.0 copy-done
  1.3 0.0 slice-start
  1.3 1.6 convolution_convert_fusion
  2.9 0.0 slice-start.1
  2.9 71.6 %all_to_all.10 = bf16[32,24,3584]{2,1,0:T(8,128)(2,1)S(1)} all-to-all(bf16[32,24,3584]{2,1,0:T(8,128)(2,1)S(1)} %bitcast.35), channel_id=1, replica_groups=mesh['rep'=4,'exp'=32] {'exp'}, dimensions={0} | all-to-all | bytes 11010048 | tf_op jit(solution)/shard_map/all_to_all | solution.py:23
  74.5 0.0 copy-start.1
  74.5 2.5 %copy-done.1 = bf16[32,24,3584]{2,1,0:T(8,128)(2,1)} copy-done((bf16[32,24,3584]{2,1,0:T(8,128)(2,1)}, bf16[32,24,3584]{2,1,0:T(8,128)(2,1)S(1)}, u32[]{:S(2)}) %copy-start.1) | copy-done | bytes 5505048
  77.0 0.0 slice-done
  77.0 0.0 slice-done.1
  77.0 7.6 %fusion.2 = f32[768,1024]{1,0:T(8,128)} fusion(bf16[768,3584]{1,0:T(8,128)(2,1)S(1)} %bitcast.37, bf16[1,3584,1024]{2,1,0:T(8,128)(2,1)S(1)} %bitcast.40), kind=kOutput, calls=%fused_computation.2 | convolution fusion | flops 5637144576 | bytes 15990784 | tf_op jit(solution)/shard_map/dot_general | solution.py:26
  84.6 20.0 %fusion.6 = bf16[768,3584]{1,0:T(8,128)(2,1)} fusion(bf16[1,1024,3584]{2,1,0:T(8,128)(2,1)} %param.13, f32[768,1024]{1,0:T(8,128)} %fusion.2, bf16[768,3584]{1,0:T(8,128)(2,1)} %bitcast.38, bf16[1,3584,1024]{2,1,0:T(8,128)(2,1)} %param.11), kind=kOutput, calls=%fused_computation.7 | convolution fusion | flops 11281760256 | bytes 28835840 | tf_op jit(solution)/shard_map/dot_general | solution.py:28
  104.6 0.0 copy-start.2
  104.6 0.0 copy-start.3
  104.6 0.0 copy-start.4
  104.6 6.4 %all-to-all-start.1 = ((bf16[32,24,3584]{2,1,0:T(8,128)(2,1)}), bf16[32,24,3584]{2,1,0:T(8,128)(2,1)}, u32[]{:S(2)}, u32[]{:S(2)}) async-start(bf16[32,24,3584]{2,1,0:T(8,128)(2,1)} %bitcast.36), calls=%async_computation.1 | async-start | bytes 11010048 | tf_op jit(solution)/shard_map/all_to_all | solution.py:29
  111.0 0.0 copy-done.2
  111.0 0.0 copy-done.3
  111.1 0.0 copy-done.4
  111.1 0.1 fusion.27
  111.2 74.6 %all-to-all-done.1 = bf16[32,24,3584]{2,1,0:T(8,128)(2,1)} async-done(((bf16[32,24,3584]{2,1,0:T(8,128)(2,1)}), bf16[32,24,3584]{2,1,0:T(8,128)(2,1)}, u32[]{:S(2)}, u32[]{:S(2)}) %all-to-all-start.1) | async-done | bytes 5505056 | tf_op jit(solution)/shard_map/all_to_all | solution.py:29
  185.8 3.5 %convolution_bitcast_fusion = f32[128,3584]{1,0:T(8,128)S(1)} fusion(bf16[32,24,3584]{2,1,0:T(8,128)(2,1)} %all-to-all-done.1, s32[32,128]{1,0:T(8,128)S(1)} %fusion.16, bf16[32,128]{1,0:T(8,128)(2,1)S(1)} %get-tuple-element.5), kind=kOutput, calls=%fused_computation.8 | convolution fusion | flops 704839680 | bytes 7364608 | tf_op jit(solution)/shard_map/dot_general | solution.py:38
  189.2 4.4 %fusion.10 = bf16[128,3584]{1,0:T(8,128)(2,1)} fusion(f32[128,3584]{1,0:T(8,128)S(1)} %convolution_bitcast_fusion, bf16[32,24,3584]{2,1,0:T(8,128)(2,1)} %all-to-all-done.1, s32[32,128]{1,0:T(8,128)S(1)} %fusion.16, bf16[32,128]{1,0:T(8,128)(2,1)S(1)} %get-tuple-element.6), kind=kOutput, calls=%fused_computation.11 | convolution fusion | flops 705757184 | bytes 8282112 | tf_op jit(solution)/shard_map/dot_general | solution.py:37
  (3 shorter events, 0.0 us)
Async XLA Ops:
  0.0 1.3 copy-start
  1.3 75.7 %slice-start = ((s8[7340032]{0:T(1024)(128)(4,1)}), s8[4194304]{0:T(1024)(128)(4,1)S(1)}, s32[]{:S(2)}) async-start(s8[7340032]{0:T(1024)(128)(4,1)} %bitcast.39), calls=%async_computation.2 | async-start | bytes 8388608
  2.9 74.1 %slice-start.1 = ((s8[7340032]{0:T(1024)(128)(4,1)}), s8[3145728]{0:T(1024)(128)(4,1)S(1)}, s32[]{:S(2)}) async-start(s8[7340032]{0:T(1024)(128)(4,1)} %bitcast.39), calls=%async_computation.3 | async-start | bytes 6291456
  74.5 2.5 %copy-start.1 = (bf16[32,24,3584]{2,1,0:T(8,128)(2,1)}, bf16[32,24,3584]{2,1,0:T(8,128)(2,1)S(1)}, u32[]{:S(2)}) copy-start(bf16[32,24,3584]{2,1,0:T(8,128)(2,1)S(1)} %all_to_all.10) | copy-start | bytes 16515076
  104.6 6.4 %copy-start.2 = (s32[128,4]{0,1:T(4,128)S(1)}, s32[128,4]{0,1:T(4,128)}, u32[]{:S(2)}) copy-start(s32[128,4]{0,1:T(4,128)} %param.8) | copy-start | bytes 6148
  104.6 6.4 %copy-start.3 = (f32[128,4]{0,1:T(4,128)S(1)}, f32[128,4]{0,1:T(4,128)}, u32[]{:S(2)}) copy-start(f32[128,4]{0,1:T(4,128)} %param.9) | copy-start | bytes 6148
  104.6 6.4 %copy-start.4 = (s32[32]{0:T(128)S(1)}, s32[32]{0:T(128)}, u32[]{:S(2)}) copy-start(s32[32]{0:T(128)} %param.10) | copy-start | bytes 388
  104.6 81.1 %all-to-all-start.1 = ((bf16[32,24,3584]{2,1,0:T(8,128)(2,1)}), bf16[32,24,3584]{2,1,0:T(8,128)(2,1)}, u32[]{:S(2)}, u32[]{:S(2)}) async-start(bf16[32,24,3584]{2,1,0:T(8,128)(2,1)} %bitcast.36), calls=%async_computation.1 | async-start | bytes 11010048 | tf_op jit(solution)/shard_map/all_to_all | solution.py:29
